TPU v7x, 128 devices: a whole 4x4x4 slice. The times are simulated.
128 devices in a mesh: px: 8 (over x, core), py: 16 (over y, z).
Axes of the slice: x: 4, y: 4, z: 4, core: 2. Of those that a mesh axis runs over, the one named last changes fastest.
Arguments:
- root_density: float32 [384, 384, 384], P('px', 'py'), may hold values from -6 to 6
- subgrid_density: float32 [2048, 32, 1024], P(('px', 'py')), may hold values from -24 to 24
- velocity: float32 [3, 2048, 32, 1024], P(None, ('px', 'py')), may hold values from -6 to 6
- slot_anchor: int32 [3, 2048], replicated, may hold values from 0 to 376, as said below
- slot_count: int32 [128], replicated, may hold values from 1 to 16, as said below
- neighbour: int32 [2, 2048], replicated, may hold values from -1 to 2047, as said below
Outputs:
- coarse_potential: float32 [384, 384, 384], P('px', 'py')
- subgrid_potential: float32 [2048, 32, 1024], P(('px', 'py'))
- kicked_velocity: float32 [3, 2048, 32, 1024], P(None, ('px', 'py'))
Inputs may be any that keep to these rules, and one draw needn't show every extreme that they name: Slot j of device d is slot d * 16 + j, devices numbered in the order of px+py; it is live when j < slot_count[d]. Some device has every slot live. `slot_anchor`: entries are multiples of 8; live slots cover distinct regions of 8^3 root cells; empty slots hold 0. The region of live slot j of the device at px = p, py = q has its lower corner among the root cells that the device at px = p, py = (q + j) mod 16 holds of root_density. neighbour[0, s] is s - 16 or -1 and neighbour[1, s] is s + 16 or -1, the same slot of the device one index lower or higher along py with the same px; where set, both slots are live and the two regions lie next to each other along the second dimension, the lower one below. Empty slots hold -1.
All inputs are finite; a program needn't handle non-finite values.
Results may differ from a plain program's by a relative error of at most 0.000094.
Values sent between devices are 32-bit elements; how exact they have to be, the bound alone decides.
No kernel may reach another device: no remote copies, remote signals or barrier semaphores. Data moves between devices by JAX's collectives and lax.ppermute only.
A program may use at most 128 MiB of HBM per device.

v0:
```python
import jax
import jax.numpy as jnp
from jax import lax
from jax.sharding import PartitionSpec as P

NR = 384
REG = 8
REF = 4
SWEEPS = 4
HIGHEST_PRECISION = lax.Precision.HIGHEST
RELAXATION = 6.0 / 7.0
EINSUM_FORMS = ("abc,ad->dbc", "abc,bd->adc", "abc,cd->abd")


def from_behind(value, axis, steps):
    count = lax.axis_size(axis)
    initial, last = (max(0, -steps), min(count, count - steps))
    return lax.ppermute(value, axis, [(source, source + steps) for source in range(initial, last)])


def extended(block, sides, width):
    for axis, dim in sides:
        count = lax.axis_size(axis)
        forward = [(i, i + 1) for i in range(count - 1)]
        forward.append((count - 1, 0))
        backward = [(target, source) for source, target in forward]
        low = lax.ppermute(
            lax.slice_in_dim(block, block.shape[dim] - width, None, axis=dim), axis, forward
        )
        high = lax.ppermute(lax.slice_in_dim(block, 0, width, axis=dim), axis, backward)
        block = jnp.concatenate([low, block, high], axis=dim)
    return block


def tables(length):
    positions = jnp.arange(length, dtype=jnp.int32)
    angle_table = (
        2.0
        * jnp.pi
        / length
        * (positions[:, None] * positions[None, :] % length).astype(jnp.float32)
    )
    return (jnp.cos(angle_table), jnp.sin(angle_table))


def transform_along(values_in, matrix, axis_number):
    return jnp.einsum(EINSUM_FORMS[axis_number], values_in, matrix, precision=HIGHEST_PRECISION)


def forward(complex_pair, axis_number, cosine_table, sine_table):
    real_part, imag_part = complex_pair
    return (
        transform_along(real_part, cosine_table, axis_number)
        + transform_along(imag_part, sine_table, axis_number),
        transform_along(imag_part, cosine_table, axis_number)
        - transform_along(real_part, sine_table, axis_number),
    )


def inverse(complex_pair, axis_number, cosine_table, sine_table):
    real_part, imag_part = complex_pair
    scale_factor = 1.0 / cosine_table.shape[0]
    return (
        (
            transform_along(real_part, cosine_table, axis_number)
            - transform_along(imag_part, sine_table, axis_number)
        )
        * scale_factor,
        (
            transform_along(imag_part, cosine_table, axis_number)
            + transform_along(real_part, sine_table, axis_number)
        )
        * scale_factor,
    )


def eigenvalue(wavenumber):
    return -4.0 * jnp.sin(jnp.pi / NR * wavenumber.astype(jnp.float32)) ** 2


def green_block(wave_first, wave_second, wave_third):
    total = (
        eigenvalue(wave_first)[:, None, None]
        + eigenvalue(wave_second)[None, :, None]
        + eigenvalue(wave_third)[None, None, :]
    )
    zero_mode = (
        (wave_first[:, None, None] == 0)
        & (wave_second[None, :, None] == 0)
        & (wave_third[None, None, :] == 0)
    )
    safe_total = jnp.where(zero_mode, -1.0, total)
    return jnp.where(zero_mode, 0.0, 1.0 / safe_total)


def weights_table():
    cells = jnp.arange(REG * REF + 2, dtype=jnp.int32)
    marks = 2 * cells - 1 + REF
    lower_cell = jnp.minimum(marks // (2 * REF), REG)
    fraction = (marks - 2 * REF * lower_cell).astype(jnp.float32) / (2 * REF)
    columns = jnp.arange(REG + 2, dtype=jnp.int32)
    return jnp.where(
        columns[None, :] == lower_cell[:, None], 1.0 - fraction[:, None], 0.0
    ) + jnp.where(columns[None, :] == lower_cell[:, None] + 1, fraction[:, None], 0.0)


def coarse_parts(patch_flat, weights):
    inner = weights[1:-1]
    cells = inner.shape[0]
    width = weights.shape[1]
    both_inner = jnp.einsum("jb,kc->jkbc", inner, inner, precision=HIGHEST_PRECISION).reshape(
        cells * cells, width * width
    )
    second_low = jnp.einsum("b,kc->kbc", weights[0], inner, precision=HIGHEST_PRECISION).reshape(
        cells, width * width
    )
    second_high = jnp.einsum("b,kc->kbc", weights[-1], inner, precision=HIGHEST_PRECISION).reshape(
        cells, width * width
    )
    third_low = jnp.einsum("jb,c->jbc", inner, weights[0], precision=HIGHEST_PRECISION).reshape(
        cells, width * width
    )
    third_high = jnp.einsum("jb,c->jbc", inner, weights[-1], precision=HIGHEST_PRECISION).reshape(
        cells, width * width
    )
    plane_values = jnp.einsum("sam,nm->san", patch_flat, both_inner, precision=HIGHEST_PRECISION)
    interior = jnp.einsum("san,ia->sin", plane_values, inner, precision=HIGHEST_PRECISION)
    first_low_face = jnp.einsum("san,a->sn", plane_values, weights[0], precision=HIGHEST_PRECISION)
    first_high_face = jnp.einsum(
        "san,a->sn", plane_values, weights[-1], precision=HIGHEST_PRECISION
    )

    def face_of(table):
        partial_face = jnp.einsum("sam,km->sak", patch_flat, table, precision=HIGHEST_PRECISION)
        return jnp.einsum("sak,ia->sik", partial_face, inner, precision=HIGHEST_PRECISION)

    return (
        interior,
        first_low_face,
        first_high_face,
        face_of(second_low),
        face_of(second_high),
        face_of(third_low),
        face_of(third_high),
    )


def spread_third(face_values, cells, corner):
    positions = jnp.arange(cells * cells, dtype=jnp.int32)
    rows = jnp.arange(cells, dtype=jnp.int32)
    placer = (positions[None, :] == rows[:, None] * cells + corner).astype(jnp.float32)
    return jnp.einsum("sij,jn->sin", face_values, placer, precision=HIGHEST_PRECISION)


def beside_values(interior, first_faces, second_faces, third_full, third_place):
    cells = interior.shape[1]
    slots = interior.shape[0]
    first_low, first_high = first_faces
    second_low, second_high = second_faces
    third_low, third_high = third_full
    below_first = jnp.concatenate([first_low[:, None, :], interior[:, :-1]], axis=1)
    above_first = jnp.concatenate([interior[:, 1:], first_high[:, None, :]], axis=1)
    below_second = jnp.concatenate([second_low, interior[:, :, :-cells]], axis=2)
    above_second = jnp.concatenate([interior[:, :, cells:], second_high], axis=2)
    zero_column = jnp.zeros((slots, cells, 1), jnp.float32)
    below_third = jnp.where(
        third_place == 0, third_low, jnp.concatenate([zero_column, interior[:, :, :-1]], axis=2)
    )
    above_third = jnp.where(
        third_place == cells - 1,
        third_high,
        jnp.concatenate([interior[:, :, 1:], zero_column], axis=2),
    )
    return ((below_first, above_first), (below_second, above_second), (below_third, above_third))


def cut_patches(padded, anchors, corner_first, corner_second):
    offsets = jnp.arange(REG + 2, dtype=jnp.int32)
    index_first = jnp.clip(
        anchors[0][:, None] - corner_first + offsets[None, :], 0, padded.shape[0] - 1
    )
    index_second = jnp.clip(
        anchors[1][:, None] - corner_second + offsets[None, :], 0, padded.shape[1] - 1
    )
    index_third = (anchors[2][:, None] - 1 + offsets[None, :]) % NR
    picked = padded[
        index_first[:, :, None, None], index_second[:, None, :, None], index_third[:, None, None, :]
    ]
    return picked.reshape(anchors.shape[1], -1)


def neighbour_faces(interior):
    cells = interior.shape[1]
    top_layer = interior[:, :, (cells - 1) * cells :]
    bottom_layer = interior[:, :, :cells]
    from_below = from_behind(top_layer, "py", 1)
    from_above = from_behind(bottom_layer, "py", -1)
    return (from_below, from_above)


def local(root_density, subgrid_density, velocity, slot_anchor, slot_count, neighbour):
    cosine_table, sine_table = tables(NR)
    first_rows = root_density.shape[0]
    second_rows = root_density.shape[1]
    size_second = lax.axis_size("py")
    place_first = lax.axis_index("px")
    place_second = lax.axis_index("py")
    device = place_first * size_second + place_second
    every_wave = jnp.arange(NR, dtype=jnp.int32)
    real_part = transform_along(root_density, cosine_table, 2)
    imag_part = -transform_along(root_density, sine_table, 2)
    spectrum = (
        lax.all_to_all(real_part, "py", split_axis=0, concat_axis=1, tiled=True),
        lax.all_to_all(imag_part, "py", split_axis=0, concat_axis=1, tiled=True),
    )
    spectrum = forward(spectrum, 1, cosine_table, sine_table)
    spectrum = (
        lax.all_to_all(spectrum[0], ("px", "py"), split_axis=1, concat_axis=0, tiled=True),
        lax.all_to_all(spectrum[1], ("px", "py"), split_axis=1, concat_axis=0, tiled=True),
    )
    band = spectrum[0].shape[1]
    band_start = device * band
    spectrum = forward(spectrum, 0, cosine_table, sine_table)
    factor = green_block(every_wave, band_start + jnp.arange(band, dtype=jnp.int32), every_wave)
    spectrum = inverse((spectrum[0] * factor, spectrum[1] * factor), 0, cosine_table, sine_table)
    spectrum = (
        lax.all_to_all(spectrum[0], ("px", "py"), split_axis=0, concat_axis=1, tiled=True),
        lax.all_to_all(spectrum[1], ("px", "py"), split_axis=0, concat_axis=1, tiled=True),
    )
    spectrum = inverse(spectrum, 1, cosine_table, sine_table)
    spectrum = (
        lax.all_to_all(spectrum[0], "py", split_axis=1, concat_axis=0, tiled=True),
        lax.all_to_all(spectrum[1], "py", split_axis=1, concat_axis=0, tiled=True),
    )
    coarse_potential = (
        transform_along(spectrum[0], cosine_table, 2) - transform_along(spectrum[1], sine_table, 2)
    ) * (1.0 / NR)
    per_device = subgrid_density.shape[0]
    cells = subgrid_density.shape[1]
    positions = jnp.arange(per_device, dtype=jnp.int32)
    corner_first = place_first * first_rows
    corner_second = place_second * second_rows
    padded = extended(coarse_potential, (("px", 0), ("py", 1)), 1)
    targets = jnp.arange(size_second, dtype=jnp.int32)
    owner_devices = place_first * size_second + targets
    wanted_slot = (place_second - targets) % size_second
    global_slot = owner_devices * per_device + wanted_slot
    sending_live = wanted_slot < slot_count[owner_devices]
    sending = cut_patches(padded, slot_anchor[:, global_slot], corner_first, corner_second)
    sending = jnp.where(sending_live[:, None], sending, 0.0)
    arrived = lax.all_to_all(sending, "py", split_axis=0, concat_axis=0, tiled=True)
    patch = arrived[(place_second + positions) % size_second]
    patch_flat = patch.reshape(per_device, REG + 2, (REG + 2) * (REG + 2))
    interior, first_low, first_high, second_low, second_high, third_low, third_high = coarse_parts(
        patch_flat, weights_table()
    )
    third_full = (spread_third(third_low, cells, 0), spread_third(third_high, cells, cells - 1))
    third_place = jnp.arange(cells * cells, dtype=jnp.int32) % cells
    own_live = positions < slot_count[device]
    first_slot = device * per_device
    nearby = lax.dynamic_slice_in_dim(neighbour, first_slot, per_device, 1)
    use_below = (nearby[0] >= 0)[:, None, None]
    use_above = (nearby[1] >= 0)[:, None, None]

    def all_beside(current):
        from_below, from_above = neighbour_faces(current)
        second_faces = (
            jnp.where(use_below, from_below, second_low),
            jnp.where(use_above, from_above, second_high),
        )
        return beside_values(
            current, (first_low, first_high), second_faces, third_full, third_place
        )

    for sweep_index in range(SWEEPS):
        along_first, along_second, along_third = all_beside(interior)
        beside_all = (
            along_first[1]
            + along_first[0]
            + along_second[1]
            + along_second[0]
            + along_third[1]
            + along_third[0]
        )
        interior = (1.0 - RELAXATION) * interior + RELAXATION * (
            beside_all - subgrid_density * (1.0 / (REF * REF))
        ) / 6.0
    along_first, along_second, along_third = all_beside(interior)
    scale_factor = REF / 2.0
    slopes = jnp.stack(
        [
            (along_first[1] - along_first[0]) * scale_factor,
            (along_second[1] - along_second[0]) * scale_factor,
            (along_third[1] - along_third[0]) * scale_factor,
        ]
    )
    subgrid_potential = jnp.where(own_live[:, None, None], interior, 0.0)
    velocity_after_kick = jnp.where(own_live[None, :, None, None], velocity - slopes, 0.0)
    return (coarse_potential, subgrid_potential, velocity_after_kick)


def solution(mesh):
    return jax.shard_map(
        local,
        mesh=mesh,
        in_specs=(
            P("px", "py", None),
            P(("px", "py"), None, None),
            P(None, ("px", "py"), None, None),
            P(),
            P(),
            P(),
        ),
        out_specs=(
            P("px", "py", None),
            P(("px", "py"), None, None),
            P(None, ("px", "py"), None, None),
        ),
        check_vma=False,
    )
```

profile of v0, /device:TPU:96, one launch (start us, length us, event | category | flops | bytes accessed | tf_op | source)
XLA Modules:
  0.0 679.2 jit_solution(3072733215062630244)
XLA Ops:
  2.1 5.8 negate_bitcast_fusion
  9.6 7.8 %all-to-all-start.1 = ((f32[48,24,384]{2,1,0:T(8,128)}), f32[48,24,384]{2,1,0:T(8,128)S(1)}, u32[]{:S(2)}, u32[]{:S(2)}) async-start(f32[48,24,384]{2,1,0:T(8,128)} %copy.93), calls=%async_computation.1 | async-start | bytes 3538944 | tf_op jit(solution)/shard_map/all_to_all | solution.py:214
  17.4 5.8 fusion.38
  24.9 15.3 %all-to-all-done.1 = f32[48,24,384]{2,1,0:T(8,128)S(1)} async-done(((f32[48,24,384]{2,1,0:T(8,128)}), f32[48,24,384]{2,1,0:T(8,128)S(1)}, u32[]{:S(2)}, u32[]{:S(2)}) %all-to-all-start.1) | async-done | bytes 1769504 | tf_op jit(solution)/shard_map/all_to_all | solution.py:214
  40.2 7.7 %all-to-all-start = ((f32[48,24,384]{2,1,0:T(8,128)}), f32[48,24,384]{2,1,0:T(8,128)}, u32[]{:S(2)}, u32[]{:S(2)}) async-start(f32[48,24,384]{2,1,0:T(8,128)} %copy.89), calls=%async_computation | async-start | bytes 3538944 | tf_op jit(solution)/shard_map/all_to_all | solution.py:213
  48.1 21.4 %all-to-all-done = f32[48,24,384]{2,1,0:T(8,128)} async-done(((f32[48,24,384]{2,1,0:T(8,128)}), f32[48,24,384]{2,1,0:T(8,128)}, u32[]{:S(2)}, u32[]{:S(2)}) %all-to-all-start) | async-done | bytes 1769504 | tf_op jit(solution)/shard_map/all_to_all | solution.py:213
  71.0 5.3 fusion.71
  76.3 5.4 add_bitcast_fusion
  81.7 3.0 copy.96
  84.7 9.3 %all-to-all-start.2 = ((f32[3,384,384]{2,0,1:T(4,128)}), f32[3,384,384]{2,0,1:T(4,128)}, u32[]{:S(2)}, u32[]{:S(2)}) async-start(f32[3,384,384]{2,0,1:T(4,128)} %copy.96), calls=%async_computation.2 | async-start | bytes 4718592 | tf_op jit(solution)/shard_map/all_to_all | solution.py:218
  94.1 5.3 fusion.66
  99.4 5.4 subtract_bitcast_fusion
  104.8 2.8 copy.102
  107.6 17.3 %all-to-all-done.2 = f32[3,384,384]{2,0,1:T(4,128)} async-done(((f32[3,384,384]{2,0,1:T(4,128)}), f32[3,384,384]{2,0,1:T(4,128)}, u32[]{:S(2)}, u32[]{:S(2)}) %all-to-all-start.2) | async-done | bytes 1769504 | tf_op jit(solution)/shard_map/all_to_all | solution.py:218
  124.8 6.2 all-to-all-start.3
  131.3 3.5 copy.98
  134.8 4.1 all_to_all.121
  138.9 23.2 %all-to-all-done.3 = f32[3,384,384]{2,0,1:T(4,128)S(1)} async-done(((f32[3,384,384]{2,0,1:T(4,128)}), f32[3,384,384]{2,0,1:T(4,128)S(1)}, u32[]{:S(2)}, u32[]{:S(2)}) %all-to-all-start.3) | async-done | bytes 1769504 | tf_op jit(solution)/shard_map/all_to_all | solution.py:219
  163.8 2.9 all_to_all.125
  166.7 5.3 fusion.64
  172.1 5.3 fusion.73
  177.4 6.2 subtract_multiply_fusion.2
  183.6 5.8 add_multiply_fusion.1
  189.4 5.5 fusion.62
  194.9 5.4 add_multiply_fusion
  202.9 6.6 all-to-all-start.5
  209.5 6.9 %fusion.75 = f32[384,3,384]{2,0,1:T(8,128)S(1)} fusion(f32[384,3,384]{2,0,1:T(8,128)} %copy-done.8), kind=kOutput, calls=%fused_computation.115 | convolution fusion | flops 2039758848 | bytes 3538944 | tf_op jit(solution)/shard_map/abc,ad->dbc/dot_general | solution.py:47
  216.4 5.4 subtract_multiply_fusion.1
  221.8 2.8 copy.110
  224.6 15.5 %all-to-all-done.5 = f32[384,3,384]{2,1,0:T(4,128)S(1)} async-done(((f32[384,3,384]{2,1,0:T(4,128)}), f32[384,3,384]{2,1,0:T(4,128)S(1)}, u32[]{:S(2)}, u32[]{:S(2)}) %all-to-all-start.5) | async-done | bytes 1769504 | tf_op jit(solution)/shard_map/all_to_all | solution.py:228
  240.1 7.0 %all-to-all-start.4 = ((f32[384,3,384]{2,1,0:T(4,128)}), f32[384,3,384]{2,1,0:T(4,128)}, u32[]{:S(2)}, u32[]{:S(2)}) async-start(f32[384,3,384]{2,1,0:T(4,128)} %copy.110), calls=%async_computation.4 | async-start | bytes 4718592 | tf_op jit(solution)/shard_map/all_to_all | solution.py:227
  252.9 2.9 all_to_all.133
  255.7 22.1 %all-to-all-done.4 = f32[384,3,384]{2,1,0:T(4,128)} async-done(((f32[384,3,384]{2,1,0:T(4,128)}), f32[384,3,384]{2,1,0:T(4,128)}, u32[]{:S(2)}, u32[]{:S(2)}) %all-to-all-start.4) | async-done | bytes 1769504 | tf_op jit(solution)/shard_map/all_to_all | solution.py:227
  277.8 3.5 copy.112
  281.3 2.9 all_to_all.129
  284.2 5.3 fusion.60
  289.5 5.4 multiply_bitcast_fusion.1
  294.9 3.0 copy.124
  297.9 5.9 all-to-all-start.7
  309.2 5.3 fusion.77
  314.5 5.4 multiply_bitcast_fusion.2
  322.7 11.2 %all-to-all-done.7 = f32[3,384,384]{2,0,1:T(4,128)} async-done(((f32[3,384,384]{2,0,1:T(4,128)}), f32[3,384,384]{2,0,1:T(4,128)}, u32[]{:S(2)}, u32[]{:S(2)}) %all-to-all-start.7) | async-done | bytes 1769504 | tf_op jit(solution)/shard_map/all_to_all | solution.py:233
  333.9 6.9 %all-to-all-start.6 = ((f32[3,384,384]{2,0,1:T(4,128)}), f32[3,384,384]{2,0,1:T(4,128)S(1)}, u32[]{:S(2)}, u32[]{:S(2)}) async-start(f32[3,384,384]{2,0,1:T(4,128)} %copy.120), calls=%async_computation.6 | async-start | bytes 4718592 | tf_op jit(solution)/shard_map/all_to_all | solution.py:232
  345.4 3.0 copy.125
  348.4 20.7 %all-to-all-done.6 = f32[3,384,384]{2,0,1:T(4,128)S(1)} async-done(((f32[3,384,384]{2,0,1:T(4,128)}), f32[3,384,384]{2,0,1:T(4,128)S(1)}, u32[]{:S(2)}, u32[]{:S(2)}) %all-to-all-start.6) | async-done | bytes 1769504 | tf_op jit(solution)/shard_map/all_to_all | solution.py:232
  369.2 5.8 fusion.68
  375.0 6.3 subtract_multiply_fusion
  381.4 2.9 collective-permute-start.1
  389.8 3.0 reshape.606
  397.3 3.0 collective-permute-done.3
  402.2 151.5 %gather_fusion.2 = f32[16000]{0:T(1024)S(1)} fusion(f32[50,26,384]{2,1,0:T(8,128)S(1)} %pad_maximum_fusion.8, s32[16000]{0:T(1024)S(1)} %reshape.573), kind=kCustom, calls=%fused_computation.2 | custom fusion | bytes 320000 | tf_op jit(solution)/shard_map/gather | solution.py:186
  554.6 9.3 %all-to-all-start.8 = ((f32[16,1,1000]{2,1,0:T(1,128)}), f32[16,1,1000]{2,1,0:T(1,128)S(1)}, u32[]{:S(2)}, u32[]{:S(2)}) async-start(f32[16,1,1000]{2,1,0:T(1,128)} %broadcast_select_fusion.1), calls=%async_computation.8 | async-start | bytes 131072 | tf_op jit(solution)/shard_map/all_to_all | solution.py:251
  564.5 5.1 all-to-all-done.8
  584.9 5.5 collective-permute-start.5
  599.0 6.5 collective-permute-start.7
  609.4 7.3 %collective-permute-done.6 = f32[16,32,32]{2,1,0:T(8,128)S(1)} collective-permute-done((f32[16,32,32]{2,1,0:T(8,128)S(1)}, f32[16,32,32]{2,1,0:T(8,128)S(1)}, u32[]{:S(2)}, u32[]{:S(2)}) %collective-permute-start.6) | collective-permute-done | bytes 65568 | tf_op jit(solution)/shard_map/ppermute | solution.py:18
  616.8 3.1 fusion.15
  623.9 6.0 collective-permute-start.9
  633.9 3.0 broadcast_multiply_fusion
  641.0 6.7 collective-permute-start.11
  651.4 4.0 broadcast_select_fusion
  657.7 6.5 collective-permute-start.13
  668.2 6.4 collective-permute-done.12
  675.4 3.5 fusion
  (197 shorter events, 93.5 us)
Async XLA Ops:
  0.6 1.5 copy-start
  9.6 30.6 %all-to-all-start.1 = ((f32[48,24,384]{2,1,0:T(8,128)}), f32[48,24,384]{2,1,0:T(8,128)S(1)}, u32[]{:S(2)}, u32[]{:S(2)}) async-start(f32[48,24,384]{2,1,0:T(8,128)} %copy.93), calls=%async_computation.1 | async-start | bytes 3538944 | tf_op jit(solution)/shard_map/all_to_all | solution.py:214
  40.2 29.3 %all-to-all-start = ((f32[48,24,384]{2,1,0:T(8,128)}), f32[48,24,384]{2,1,0:T(8,128)}, u32[]{:S(2)}, u32[]{:S(2)}) async-start(f32[48,24,384]{2,1,0:T(8,128)} %copy.89), calls=%async_computation | async-start | bytes 3538944 | tf_op jit(solution)/shard_map/all_to_all | solution.py:213
  84.7 40.1 %all-to-all-start.2 = ((f32[3,384,384]{2,0,1:T(4,128)}), f32[3,384,384]{2,0,1:T(4,128)}, u32[]{:S(2)}, u32[]{:S(2)}) async-start(f32[3,384,384]{2,0,1:T(4,128)} %copy.96), calls=%async_computation.2 | async-start | bytes 4718592 | tf_op jit(solution)/shard_map/all_to_all | solution.py:218
  124.8 37.2 %all-to-all-start.3 = ((f32[3,384,384]{2,0,1:T(4,128)}), f32[3,384,384]{2,0,1:T(4,128)S(1)}, u32[]{:S(2)}, u32[]{:S(2)}) async-start(f32[3,384,384]{2,0,1:T(4,128)} %copy.102), calls=%async_computation.3 | async-start | bytes 4718592 | tf_op jit(solution)/shard_map/all_to_all | solution.py:219
  166.7 5.3 copy-start.5
  183.6 5.8 copy-start.6
  189.4 5.5 copy-start.8
  202.9 37.2 %all-to-all-start.5 = ((f32[384,3,384]{2,1,0:T(4,128)}), f32[384,3,384]{2,1,0:T(4,128)S(1)}, u32[]{:S(2)}, u32[]{:S(2)}) async-start(f32[384,3,384]{2,1,0:T(4,128)} %copy.116), calls=%async_computation.5 | async-start | bytes 4718592 | tf_op jit(solution)/shard_map/all_to_all | solution.py:228
  209.5 6.9 %copy-start.7 = (f32[384,3,384]{2,0,1:T(8,128)S(1)}, f32[384,3,384]{2,0,1:T(8,128)}, u32[]{:S(2)}) copy-start(f32[384,3,384]{2,0,1:T(8,128)} %copy-done.6) | copy-start | bytes 5308420
  224.6 22.5 %copy-start.19 = (s32[3,2048]{1,0:T(4,128)S(1)}, s32[3,2048]{1,0:T(4,128)}, u32[]{:S(2)}) copy-start(s32[3,2048]{1,0:T(4,128)} %param.9) | copy-start | bytes 73732
  224.6 22.9 %copy-start.2 = (s32[128]{0:T(128)S(1)}, s32[128]{0:T(128)}, u32[]{:S(2)}) copy-start(s32[128]{0:T(128)} %param.10) | copy-start | bytes 1540
  240.1 37.7 %all-to-all-start.4 = ((f32[384,3,384]{2,1,0:T(4,128)}), f32[384,3,384]{2,1,0:T(4,128)}, u32[]{:S(2)}, u32[]{:S(2)}) async-start(f32[384,3,384]{2,1,0:T(4,128)} %copy.110), calls=%async_computation.4 | async-start | bytes 4718592 | tf_op jit(solution)/shard_map/all_to_all | solution.py:227
  297.9 36.0 %all-to-all-start.7 = ((f32[3,384,384]{2,0,1:T(4,128)}), f32[3,384,384]{2,0,1:T(4,128)}, u32[]{:S(2)}, u32[]{:S(2)}) async-start(f32[3,384,384]{2,0,1:T(4,128)} %copy.124), calls=%async_computation.7 | async-start | bytes 4718592 | tf_op jit(solution)/shard_map/all_to_all | solution.py:233
  305.7 35.9 %copy-start.11 = (f32[34,10]{0,1:T(8,128)}, f32[34,10]{0,1:T(8,128)S(1)}, u32[]{:S(2)}) copy-start(f32[34,10]{0,1:T(8,128)S(1)} %select_add_fusion) | copy-start | bytes 4084
  306.5 36.0 %copy-start.22 = (f32[10]{0:T(128)}, f32[10]{0:T(128)S(1)}, u32[]{:S(2)}) copy-start(f32[10]{0:T(128)S(1)} %get-tuple-element.4) | copy-start | bytes 124
  322.7 19.5 %copy-start.28 = (s32[16]{0:T(128)S(1)}, s32[16]{0:T(128)}, u32[]{:S(2)}) copy-start(s32[16]{0:T(128)} %get-tuple-element.5) | copy-start | bytes 196
  322.7 19.6 %copy-start.27 = (s32[16]{0:T(128)S(1)}, s32[16]{0:T(128)}, u32[]{:S(2)}) copy-start(s32[16]{0:T(128)} %get-tuple-element.6) | copy-start | bytes 196
  322.7 19.6 %copy-start.26 = (s32[16]{0:T(128)S(1)}, s32[16]{0:T(128)}, u32[]{:S(2)}) copy-start(s32[16]{0:T(128)} %get-tuple-element.7) | copy-start | bytes 196
  322.7 19.8 %copy-start.24 = (f32[10]{0:T(128)S(1)}, f32[10]{0:T(128)}, u32[]{:S(2)}) copy-start(f32[10]{0:T(128)} %get-tuple-element.3) | copy-start | bytes 124
  333.9 35.2 %all-to-all-start.6 = ((f32[3,384,384]{2,0,1:T(4,128)}), f32[3,384,384]{2,0,1:T(4,128)S(1)}, u32[]{:S(2)}, u32[]{:S(2)}) async-start(f32[3,384,384]{2,0,1:T(4,128)} %copy.120), calls=%async_computation.6 | async-start | bytes 4718592 | tf_op jit(solution)/shard_map/all_to_all | solution.py:232
  369.2 5.8 copy-start.9
  381.3 16.0 %copy-start.4 = (f32[48,24,384]{2,1,0:T(8,128)}, f32[48,24,384]{2,1,0:T(8,128)S(1)}, u32[]{:S(2)}) copy-start(f32[48,24,384]{2,1,0:T(8,128)S(1)} %subtract_multiply_fusion) | copy-start | bytes 5308420
  381.3 11.4 %collective-permute-start = (f32[1,24,384]{2,1,0:T(8,128)S(1)}, f32[1,24,384]{2,1,0:T(8,128)S(1)}, u32[]{:S(2)}, u32[]{:S(2)}) collective-permute-start(f32[1,24,384]{2,1,0:T(8,128)S(1)} %get-tuple-element.56), channel_id=1, source_target_pairs={{0,16},{16,32},{32,48},{48,64},{64,80},{80,96},{96,112},{112,0},{1... | collective-permute-start | bytes 110600 | tf_op jit(solution)/shard_map/ppermute | solution.py:27
  381.4 11.4 %collective-permute-start.1 = (f32[1,24,384]{2,1,0:T(8,128)S(1)}, f32[1,24,384]{2,1,0:T(8,128)S(1)}, u32[]{:S(2)}, u32[]{:S(2)}) collective-permute-start(f32[1,24,384]{2,1,0:T(8,128)S(1)} %get-tuple-element.57), channel_id=1, source_target_pairs={{16,0},{32,16},{48,32},{64,48},{80,64},{96,80},{112,96},{0,112},{1... | collective-permute-start | bytes 110600 | tf_op jit(solution)/shard_map/ppermute | solution.py:30
  392.9 4.5 collective-permute-start.2
  393.8 6.5 collective-permute-start.3
  402.1 151.7 %copy-start.29 = (pred[16]{0:T(512)(128)(4,1)S(1)}, pred[16]{0:T(512)(128)(4,1)}, u32[]{:S(2)}) copy-start(pred[16]{0:T(512)(128)(4,1)} %fusion.206) | copy-start | bytes 52
  402.2 168.5 %copy-start.10 = (f32[1024,100,1]{0,1,2:T(8,128)S(1)}, f32[1024,100,1]{0,1,2:T(8,128)}, u32[]{:S(2)}) copy-start(f32[1024,100,1]{0,1,2:T(8,128)} %reshape.606) | copy-start | bytes 1228804
  553.7 17.7 %copy-start.25 = (f32[10]{0:T(128)S(1)}, f32[10]{0:T(128)}, u32[]{:S(2)}) copy-start(f32[10]{0:T(128)} %get-tuple-element.3) | copy-start | bytes 124
  553.7 19.0 %copy-start.23 = (f32[10]{0:T(128)S(1)}, f32[10]{0:T(128)}, u32[]{:S(2)}) copy-start(f32[10]{0:T(128)} %copy-done.22) | copy-start | bytes 124
  554.6 15.1 %all-to-all-start.8 = ((f32[16,1,1000]{2,1,0:T(1,128)}), f32[16,1,1000]{2,1,0:T(1,128)S(1)}, u32[]{:S(2)}, u32[]{:S(2)}) async-start(f32[16,1,1000]{2,1,0:T(1,128)} %broadcast_select_fusion.1), calls=%async_computation.8 | async-start | bytes 131072 | tf_op jit(solution)/shard_map/all_to_all | solution.py:251
  569.7 4.3 copy-start.12
  577.9 0.8 copy-start.15
  577.9 1.1 copy-start.14
  577.9 1.3 copy-start.16
  577.9 5.4 copy-start.30
  578.7 5.6 copy-start.13
  579.5 11.6 %copy-start.20 = (pred[16]{0:T(512)(128)(4,1)S(1)}, pred[16]{0:T(512)(128)(4,1)}, u32[]{:S(2)}) copy-start(pred[16]{0:T(512)(128)(4,1)} %get-tuple-element.68) | copy-start | bytes 52
  580.5 13.7 %copy-start.21 = (pred[16]{0:T(512)(128)(4,1)S(1)}, pred[16]{0:T(512)(128)(4,1)}, u32[]{:S(2)}) copy-start(pred[16]{0:T(512)(128)(4,1)} %get-tuple-element.69) | copy-start | bytes 52
  580.5 14.1 %copy-start.3 = (f32[16,32,1024]{2,1,0:T(8,128)S(1)}, f32[16,32,1024]{2,1,0:T(8,128)}, u32[]{:S(2)}) copy-start(f32[16,32,1024]{2,1,0:T(8,128)} %param.7) | copy-start | bytes 6291460
  580.5 14.1 %copy-start.17 = (pred[1024]{0:T(1024)(128)(4,1)S(1)}, pred[1024]{0:T(1024)(128)(4,1)}, u32[]{:S(2)}) copy-start(pred[1024]{0:T(1024)(128)(4,1)} %get-tuple-element.81) | copy-start | bytes 3076
  580.5 14.1 %copy-start.18 = (pred[1024]{0:T(1024)(128)(4,1)S(1)}, pred[1024]{0:T(1024)(128)(4,1)}, u32[]{:S(2)}) copy-start(pred[1024]{0:T(1024)(128)(4,1)} %get-tuple-element.82) | copy-start | bytes 3076
  580.6 14.1 %copy-start.31 = (s32[32]{0:T(128)S(1)}, s32[32]{0:T(128)}, u32[]{:S(2)}) copy-start(s32[32]{0:T(128)} %iota_multiply_fusion) | copy-start | bytes 388
  580.6 10.5 %collective-permute-start.4 = (f32[16,32,32]{2,1,0:T(8,128)S(1)}, f32[16,32,32]{2,1,0:T(8,128)S(1)}, u32[]{:S(2)}, u32[]{:S(2)}) collective-permute-start(f32[16,32,32]{2,1,0:T(8,128)S(1)} %get-tuple-element.50), channel_id=1, source_target_pairs={{1,0},{2,1},{3,2},{4,3},{5,4},{6,5},{7,6},{8,7},{9,8},{10,9},{11,1... | collective-permute-start | bytes 196616 | tf_op jit(solution)/shard_map/ppermute | solution.py:18
  584.9 9.2 %collective-permute-start.5 = (f32[16,32,32]{2,1,0:T(8,128)S(1)}, f32[16,32,32]{2,1,0:T(8,128)S(1)}, u32[]{:S(2)}, u32[]{:S(2)}) collective-permute-start(f32[16,32,32]{2,1,0:T(8,128)S(1)} %get-tuple-element.51), channel_id=1, source_target_pairs={{0,1},{1,2},{2,3},{3,4},{4,5},{5,6},{6,7},{7,8},{8,9},{9,10},{10,1... | collective-permute-start | bytes 196616 | tf_op jit(solution)/shard_map/ppermute | solution.py:18
  599.0 10.4 %collective-permute-start.7 = (f32[16,32,32]{2,1,0:T(8,128)S(1)}, f32[16,32,32]{2,1,0:T(8,128)S(1)}, u32[]{:S(2)}, u32[]{:S(2)}) collective-permute-start(f32[16,32,32]{2,1,0:T(8,128)S(1)} %get-tuple-element.40), channel_id=1, source_target_pairs={{0,1},{1,2},{2,3},{3,4},{4,5},{5,6},{6,7},{7,8},{8,9},{9,10},{10,1... | collective-permute-start | bytes 196616 | tf_op jit(solution)/shard_map/ppermute | solution.py:18
  606.3 10.4 %collective-permute-start.6 = (f32[16,32,32]{2,1,0:T(8,128)S(1)}, f32[16,32,32]{2,1,0:T(8,128)S(1)}, u32[]{:S(2)}, u32[]{:S(2)}) collective-permute-start(f32[16,32,32]{2,1,0:T(8,128)S(1)} %get-tuple-element.41), channel_id=1, source_target_pairs={{1,0},{2,1},{3,2},{4,3},{5,4},{6,5},{7,6},{8,7},{9,8},{10,9},{11,1... | collective-permute-start | bytes 196616 | tf_op jit(solution)/shard_map/ppermute | solution.py:18
  621.5 10.4 %collective-permute-start.8 = (f32[16,32,32]{2,1,0:T(8,128)S(1)}, f32[16,32,32]{2,1,0:T(8,128)S(1)}, u32[]{:S(2)}, u32[]{:S(2)}) collective-permute-start(f32[16,32,32]{2,1,0:T(8,128)S(1)} %get-tuple-element.34), channel_id=1, source_target_pairs={{1,0},{2,1},{3,2},{4,3},{5,4},{6,5},{7,6},{8,7},{9,8},{10,9},{11,1... | collective-permute-start | bytes 196616 | tf_op jit(solution)/shard_map/ppermute | solution.py:18
  623.9 9.9 %collective-permute-start.9 = (f32[16,32,32]{2,1,0:T(8,128)S(1)}, f32[16,32,32]{2,1,0:T(8,128)S(1)}, u32[]{:S(2)}, u32[]{:S(2)}) collective-permute-start(f32[16,32,32]{2,1,0:T(8,128)S(1)} %get-tuple-element.35), channel_id=1, source_target_pairs={{0,1},{1,2},{2,3},{3,4},{4,5},{5,6},{6,7},{7,8},{8,9},{9,10},{10,1... | collective-permute-start | bytes 196616 | tf_op jit(solution)/shard_map/ppermute | solution.py:18
  638.3 10.8 %collective-permute-start.10 = (f32[16,32,32]{2,1,0:T(8,128)S(1)}, f32[16,32,32]{2,1,0:T(8,128)S(1)}, u32[]{:S(2)}, u32[]{:S(2)}) collective-permute-start(f32[16,32,32]{2,1,0:T(8,128)S(1)} %get-tuple-element.26), channel_id=1, source_target_pairs={{1,0},{2,1},{3,2},{4,3},{5,4},{6,5},{7,6},{8,7},{9,8},{10,9},{11,1... | collective-permute-start | bytes 196616 | tf_op jit(solution)/shard_map/ppermute | solution.py:18
  641.0 10.4 %collective-permute-start.11 = (f32[16,32,32]{2,1,0:T(8,128)S(1)}, f32[16,32,32]{2,1,0:T(8,128)S(1)}, u32[]{:S(2)}, u32[]{:S(2)}) collective-permute-start(f32[16,32,32]{2,1,0:T(8,128)S(1)} %get-tuple-element.27), channel_id=1, source_target_pairs={{0,1},{1,2},{2,3},{3,4},{4,5},{5,6},{6,7},{7,8},{8,9},{9,10},{10,1... | collective-permute-start | bytes 196616 | tf_op jit(solution)/shard_map/ppermute | solution.py:18
  657.7 10.4 %collective-permute-start.13 = (f32[16,32,32]{2,1,0:T(8,128)S(1)}, f32[16,32,32]{2,1,0:T(8,128)S(1)}, u32[]{:S(2)}, u32[]{:S(2)}) collective-permute-start(f32[16,32,32]{2,1,0:T(8,128)S(1)} %get-tuple-element.16), channel_id=1, source_target_pairs={{0,1},{1,2},{2,3},{3,4},{4,5},{5,6},{6,7},{7,8},{8,9},{9,10},{10,1... | collective-permute-start | bytes 196616 | tf_op jit(solution)/shard_map/ppermute | solution.py:18
  664.2 10.4 %collective-permute-start.12 = (f32[16,32,32]{2,1,0:T(8,128)S(1)}, f32[16,32,32]{2,1,0:T(8,128)S(1)}, u32[]{:S(2)}, u32[]{:S(2)}) collective-permute-start(f32[16,32,32]{2,1,0:T(8,128)S(1)} %get-tuple-element.17), channel_id=1, source_target_pairs={{1,0},{2,1},{3,2},{4,3},{5,4},{6,5},{7,6},{8,7},{9,8},{10,9},{11,1... | collective-permute-start | bytes 196616 | tf_op jit(solution)/shard_map/ppermute | solution.py:18
  667.2 8.2 %slice-start = ((s8[6291456]{0:T(1024)(128)(4,1)}), s8[4194304]{0:T(1024)(128)(4,1)S(1)}, s32[]{:S(2)}) async-start(s8[6291456]{0:T(1024)(128)(4,1)} %bitcast.255), calls=%async_computation.9 | async-start | bytes 8388608
  668.2 7.2 %slice-start.1 = ((s8[6291456]{0:T(1024)(128)(4,1)}), s8[2097152]{0:T(1024)(128)(4,1)S(1)}, s32[]{:S(2)}) async-start(s8[6291456]{0:T(1024)(128)(4,1)} %bitcast.255), calls=%async_computation.10 | async-start | bytes 4194304
  675.4 3.5 copy-start.1
where the time goes:
time: 686 us; the launch traced here: 679 us
  local copies, waits for them, and re-layouts  227 us (33%)
  waiting for transfers between devices  182 us (27%)
  matrix products  124 us (18%)
  starting transfers between devices  113 us (16%)
  other arithmetic  30.8 us (4%)
    gather x1, local copies, waits for them, and re-layouts, cut_patches(): padded[index_first[:, :, None, None], index_second[:, None, :, None], ind...  151 us
    dot_general x20, matrix products, transform_along(): jnp.einsum(EINSUM_FORMS[axis_number], values_in, matrix, precision=HIGHES...  112 us
    ppermute x10, starting transfers between devices, from_behind(): lax.ppermute(value, axis, [(source, source + steps) for source in range(i...  41.7 us
    ppermute x10, waiting for transfers between devices, from_behind(): lax.ppermute(value, axis, [(source, source + steps) for source in range(i...  25.6 us
    all_to_all x1, waiting for transfers between devices, local(): lax.all_to_all(spectrum[1], ('px', 'py'), split_axis=1, concat_axis=0, ti...  23.2 us
    all_to_all x1, waiting for transfers between devices, local(): lax.all_to_all(spectrum[0], ('px', 'py'), split_axis=0, concat_axis=1, ti...  22.1 us
    all_to_all x1, waiting for transfers between devices, local(): lax.all_to_all(real_part, 'py', split_axis=0, concat_axis=1, tiled=True)  21.4 us
    all_to_all x1, waiting for transfers between devices, local(): lax.all_to_all(spectrum[0], 'py', split_axis=1, concat_axis=0, tiled=True)  20.7 us
  transfers between devices with their start and end apart: 23, of which 21 were waited for; matrix products, arithmetic and copies ran while one was open for 13% of the time, Pallas kernels for 0%

commit v1 on v0

--- a/solution.py
+++ b/solution.py
@@ -10,6 +10,17 @@
 HIGHEST_PRECISION = lax.Precision.HIGHEST
 RELAXATION = 6.0 / 7.0
 EINSUM_FORMS = ("abc,ad->dbc", "abc,bd->adc", "abc,cd->abd")
+
+
+def in_blocks(shard, dim, peers):
+    before, after = (shard.shape[:dim], shard.shape[dim + 1 :])
+    return jnp.moveaxis(shard.reshape(*before, peers, -1, *after), dim, 0)
+
+
+def laid_out(parts, dim):
+    lengths = list(parts.shape[1:])
+    lengths[dim] *= parts.shape[0]
+    return jnp.moveaxis(parts, 0, dim).reshape(lengths)
 
 
 def from_behind(value, axis, steps):
@@ -248,7 +259,14 @@
     sending_live = wanted_slot < slot_count[owner_devices]
     sending = cut_patches(padded, slot_anchor[:, global_slot], corner_first, corner_second)
     sending = jnp.where(sending_live[:, None], sending, 0.0)
-    arrived = lax.all_to_all(sending, "py", split_axis=0, concat_axis=0, tiled=True)
+    size, index = (lax.axis_size("py"), lax.axis_index("py"))
+    blocks = in_blocks(sending, 0, size)
+    outs = [blocks[index]]
+    for step in range(1, size):
+        sent = blocks[index ^ step]
+        outs.append(lax.ppermute(sent, "py", [(i_2, i_2 ^ step) for i_2 in range(size)]))
+    blocks = jnp.stack(outs)[index ^ jnp.arange(size)]
+    arrived = laid_out(blocks, 0)
     patch = arrived[(place_second + positions) % size_second]
     patch_flat = patch.reshape(per_device, REG + 2, (REG + 2) * (REG + 2))
     interior, first_low, first_high, second_low, second_high, third_low, third_high = coarse_parts(

time: 686 us -> 699 us (1.019)
  starting transfers between devices: 113 us -> 135 us
    ppermute x0 -> x15, starting transfers between devices: none -> 31.4 us  [local(): lax.ppermute(sent, 'py', [(i_2, i_2 ^ step) for i_2 in range(size)])]
    all_to_all x1 -> x0, starting transfers between devices: 9.28 us -> none  [local(): lax.all_to_all(sending, 'py', split_axis=0, concat_axis=0, tiled=True)]
  transfers between devices with their start and end apart: 23 -> 37, of which waited for: 21 -> 20; matrix products, arithmetic and copies ran while one was open for 13% -> 12% of each run, Pallas kernels for 0% -> 0%
where the time goes in v1:
time: 699 us; the launch traced here: 693 us
  local copies, waits for them, and re-layouts  224 us (32%)
  waiting for transfers between devices  178 us (25%)
  starting transfers between devices  135 us (19%)
  matrix products  124 us (18%)
  other arithmetic  29.5 us (4%)
    gather x1, local copies, waits for them, and re-layouts, cut_patches(): padded[index_first[:, :, None, None], index_second[:, None, :, None], ind...  151 us
    dot_general x20, matrix products, transform_along(): jnp.einsum(EINSUM_FORMS[axis_number], values_in, matrix, precision=HIGHES...  112 us
    ppermute x10, starting transfers between devices, from_behind(): lax.ppermute(value, axis, [(source, source + steps) for source in range(i...  41.7 us
    ppermute x15, starting transfers between devices, local(): lax.ppermute(sent, 'py', [(i_2, i_2 ^ step) for i_2 in range(size)])  31.4 us
    ppermute x10, waiting for transfers between devices, from_behind(): lax.ppermute(value, axis, [(source, source + steps) for source in range(i...  25.6 us
    all_to_all x1, waiting for transfers between devices, local(): lax.all_to_all(spectrum[1], ('px', 'py'), split_axis=1, concat_axis=0, ti...  23.2 us
    all_to_all x1, waiting for transfers between devices, local(): lax.all_to_all(spectrum[0], ('px', 'py'), split_axis=0, concat_axis=1, ti...  22.7 us
    all_to_all x1, waiting for transfers between devices, local(): lax.all_to_all(real_part, 'py', split_axis=0, concat_axis=1, tiled=True)  21.4 us
  transfers between devices with their start and end apart: 37, of which 20 were waited for; matrix products, arithmetic and copies ran while one was open for 12% of the time, Pallas kernels for 0%

profile of v1, /device:TPU:96, one launch (start us, length us, event | category | flops | bytes accessed | tf_op | source)
XLA Modules:
  0.0 692.8 jit_solution(12589754202647125346)
XLA Ops:
  2.1 5.8 negate_bitcast_fusion
  9.6 7.8 %all-to-all-start.1 = ((f32[48,24,384]{2,1,0:T(8,128)}), f32[48,24,384]{2,1,0:T(8,128)S(1)}, u32[]{:S(2)}, u32[]{:S(2)}) async-start(f32[48,24,384]{2,1,0:T(8,128)} %copy.93), calls=%async_computation.1 | async-start | bytes 3538944 | tf_op jit(solution)/shard_map/all_to_all | solution.py:225
  17.4 5.8 fusion.38
  24.9 15.3 %all-to-all-done.1 = f32[48,24,384]{2,1,0:T(8,128)S(1)} async-done(((f32[48,24,384]{2,1,0:T(8,128)}), f32[48,24,384]{2,1,0:T(8,128)S(1)}, u32[]{:S(2)}, u32[]{:S(2)}) %all-to-all-start.1) | async-done | bytes 1769504 | tf_op jit(solution)/shard_map/all_to_all | solution.py:225
  40.2 7.7 %all-to-all-start = ((f32[48,24,384]{2,1,0:T(8,128)}), f32[48,24,384]{2,1,0:T(8,128)}, u32[]{:S(2)}, u32[]{:S(2)}) async-start(f32[48,24,384]{2,1,0:T(8,128)} %copy.89), calls=%async_computation | async-start | bytes 3538944 | tf_op jit(solution)/shard_map/all_to_all | solution.py:224
  48.1 21.4 %all-to-all-done = f32[48,24,384]{2,1,0:T(8,128)} async-done(((f32[48,24,384]{2,1,0:T(8,128)}), f32[48,24,384]{2,1,0:T(8,128)}, u32[]{:S(2)}, u32[]{:S(2)}) %all-to-all-start) | async-done | bytes 1769504 | tf_op jit(solution)/shard_map/all_to_all | solution.py:224
  71.0 5.3 fusion.71
  76.3 5.4 add_bitcast_fusion
  81.7 3.0 copy.96
  84.7 9.3 %all-to-all-start.2 = ((f32[3,384,384]{2,0,1:T(4,128)}), f32[3,384,384]{2,0,1:T(4,128)}, u32[]{:S(2)}, u32[]{:S(2)}) async-start(f32[3,384,384]{2,0,1:T(4,128)} %copy.96), calls=%async_computation.2 | async-start | bytes 4718592 | tf_op jit(solution)/shard_map/all_to_all | solution.py:229
  94.1 5.3 fusion.66
  99.4 5.4 subtract_bitcast_fusion
  107.5 17.3 %all-to-all-done.2 = f32[3,384,384]{2,0,1:T(4,128)} async-done(((f32[3,384,384]{2,0,1:T(4,128)}), f32[3,384,384]{2,0,1:T(4,128)}, u32[]{:S(2)}, u32[]{:S(2)}) %all-to-all-start.2) | async-done | bytes 1769504 | tf_op jit(solution)/shard_map/all_to_all | solution.py:229
  124.8 6.2 all-to-all-start.3
  131.3 3.5 copy.98
  134.7 4.1 all_to_all.115
  138.8 23.2 %all-to-all-done.3 = f32[3,384,384]{2,0,1:T(4,128)S(1)} async-done(((f32[3,384,384]{2,0,1:T(4,128)}), f32[3,384,384]{2,0,1:T(4,128)S(1)}, u32[]{:S(2)}, u32[]{:S(2)}) %all-to-all-start.3) | async-done | bytes 1769504 | tf_op jit(solution)/shard_map/all_to_all | solution.py:230
  163.8 2.9 all_to_all.119
  166.7 5.3 fusion.64
  172.1 5.3 fusion.73
  177.4 6.2 subtract_multiply_fusion.2
  183.6 5.8 add_multiply_fusion.1
  189.4 5.5 fusion.62
  194.9 5.4 add_multiply_fusion
  202.9 6.6 all-to-all-start.5
  209.5 6.9 fusion.75
  216.4 5.4 subtract_multiply_fusion.1
  221.8 2.8 copy.110
  224.6 15.5 %all-to-all-done.5 = f32[384,3,384]{2,1,0:T(4,128)S(1)} async-done(((f32[384,3,384]{2,1,0:T(4,128)}), f32[384,3,384]{2,1,0:T(4,128)S(1)}, u32[]{:S(2)}, u32[]{:S(2)}) %all-to-all-start.5) | async-done | bytes 1769504 | tf_op jit(solution)/shard_map/all_to_all | solution.py:239
  240.1 7.0 %all-to-all-start.4 = ((f32[384,3,384]{2,1,0:T(4,128)}), f32[384,3,384]{2,1,0:T(4,128)}, u32[]{:S(2)}, u32[]{:S(2)}) async-start(f32[384,3,384]{2,1,0:T(4,128)} %copy.110), calls=%async_computation.4 | async-start | bytes 4718592 | tf_op jit(solution)/shard_map/all_to_all | solution.py:238
  252.2 2.9 all_to_all.127
  255.1 22.7 %all-to-all-done.4 = f32[384,3,384]{2,1,0:T(4,128)} async-done(((f32[384,3,384]{2,1,0:T(4,128)}), f32[384,3,384]{2,1,0:T(4,128)}, u32[]{:S(2)}, u32[]{:S(2)}) %all-to-all-start.4) | async-done | bytes 1769504 | tf_op jit(solution)/shard_map/all_to_all | solution.py:238
  277.8 3.5 copy.112
  281.3 2.9 all_to_all.123
  284.2 5.3 fusion.60
  289.5 5.4 multiply_bitcast_fusion.1
  294.9 3.0 copy.124
  297.9 5.9 all-to-all-start.7
  309.0 5.3 fusion.77
  314.3 5.4 multiply_bitcast_fusion.2
  322.5 11.4 %all-to-all-done.7 = f32[3,384,384]{2,0,1:T(4,128)} async-done(((f32[3,384,384]{2,0,1:T(4,128)}), f32[3,384,384]{2,0,1:T(4,128)}, u32[]{:S(2)}, u32[]{:S(2)}) %all-to-all-start.7) | async-done | bytes 1769504 | tf_op jit(solution)/shard_map/all_to_all | solution.py:244
  333.9 6.9 all-to-all-start.6
  345.3 3.0 copy.125
  348.3 20.7 %all-to-all-done.6 = f32[3,384,384]{2,0,1:T(4,128)S(1)} async-done(((f32[3,384,384]{2,0,1:T(4,128)}), f32[3,384,384]{2,0,1:T(4,128)S(1)}, u32[]{:S(2)}, u32[]{:S(2)}) %all-to-all-start.6) | async-done | bytes 1769504 | tf_op jit(solution)/shard_map/all_to_all | solution.py:243
  369.1 5.8 fusion.68
  375.0 5.9 subtract_multiply_fusion
  381.0 2.9 collective-permute-start.1
  391.0 3.0 collective-permute-done.3
  395.9 151.5 %gather_fusion.2 = f32[16000]{0:T(1024)S(1)} fusion(f32[50,26,384]{2,1,0:T(8,128)S(1)} %pad_maximum_fusion.8, s32[16000]{0:T(1024)S(1)} %reshape.595), kind=kCustom, calls=%fused_computation.2 | custom fusion | bytes 320000 | tf_op jit(solution)/shard_map/gather | solution.py:197
  550.9 7.7 %collective-permute-start.16 = (f32[1,1000]{1,0:T(1,128)S(1)}, f32[1,1000]{1,0:T(1,128)S(1)}, u32[]{:S(2)}, u32[]{:S(2)}) collective-permute-start(f32[1,1000]{1,0:T(1,128)S(1)} %get-tuple-element.64), channel_id=1, source_target_pairs={{0,13},{1,12},{2,15},{3,14},{4,9},{5,8},{6,11},{7,10},{8,5},{9,4},... | collective-permute-start | bytes 12008 | tf_op jit(solution)/shard_map/ppermute | solution.py:267
  558.7 5.0 collective-permute-start.13
  563.7 4.4 collective-permute-start.11
  568.8 2.9 collective-permute-start.9
  598.4 5.7 collective-permute-start.20
  612.6 6.5 collective-permute-start.22
  623.1 7.3 %collective-permute-done.21 = f32[16,32,32]{2,1,0:T(8,128)S(1)} collective-permute-done((f32[16,32,32]{2,1,0:T(8,128)S(1)}, f32[16,32,32]{2,1,0:T(8,128)S(1)}, u32[]{:S(2)}, u32[]{:S(2)}) %collective-permute-start.21) | collective-permute-done | bytes 65568 | tf_op jit(solution)/shard_map/ppermute | solution.py:29
  630.4 3.1 fusion.15
  637.5 6.0 collective-permute-start.24
  647.5 3.0 broadcast_multiply_fusion
  654.6 6.7 collective-permute-start.26
  665.0 4.0 broadcast_select_fusion
  671.3 6.5 collective-permute-start.28
  681.8 6.4 collective-permute-done.27
  689.1 3.5 fusion
  (227 shorter events, 106.4 us)
Async XLA Ops:
  9.6 30.6 %all-to-all-start.1 = ((f32[48,24,384]{2,1,0:T(8,128)}), f32[48,24,384]{2,1,0:T(8,128)S(1)}, u32[]{:S(2)}, u32[]{:S(2)}) async-start(f32[48,24,384]{2,1,0:T(8,128)} %copy.93), calls=%async_computation.1 | async-start | bytes 3538944 | tf_op jit(solution)/shard_map/all_to_all | solution.py:225
  40.2 29.3 %all-to-all-start = ((f32[48,24,384]{2,1,0:T(8,128)}), f32[48,24,384]{2,1,0:T(8,128)}, u32[]{:S(2)}, u32[]{:S(2)}) async-start(f32[48,24,384]{2,1,0:T(8,128)} %copy.89), calls=%async_computation | async-start | bytes 3538944 | tf_op jit(solution)/shard_map/all_to_all | solution.py:224
  84.7 40.1 %all-to-all-start.2 = ((f32[3,384,384]{2,0,1:T(4,128)}), f32[3,384,384]{2,0,1:T(4,128)}, u32[]{:S(2)}, u32[]{:S(2)}) async-start(f32[3,384,384]{2,0,1:T(4,128)} %copy.96), calls=%async_computation.2 | async-start | bytes 4718592 | tf_op jit(solution)/shard_map/all_to_all | solution.py:229
  124.8 37.2 %all-to-all-start.3 = ((f32[3,384,384]{2,0,1:T(4,128)}), f32[3,384,384]{2,0,1:T(4,128)S(1)}, u32[]{:S(2)}, u32[]{:S(2)}) async-start(f32[3,384,384]{2,0,1:T(4,128)} %copy.102), calls=%async_computation.3 | async-start | bytes 4718592 | tf_op jit(solution)/shard_map/all_to_all | solution.py:230
  183.6 5.8 copy-start.7
  189.4 5.5 copy-start.9
  202.9 37.2 %all-to-all-start.5 = ((f32[384,3,384]{2,1,0:T(4,128)}), f32[384,3,384]{2,1,0:T(4,128)S(1)}, u32[]{:S(2)}, u32[]{:S(2)}) async-start(f32[384,3,384]{2,1,0:T(4,128)} %copy.116), calls=%async_computation.5 | async-start | bytes 4718592 | tf_op jit(solution)/shard_map/all_to_all | solution.py:239
  209.5 6.9 copy-start.8
  224.6 22.5 %copy-start.19 = (s32[3,2048]{1,0:T(4,128)S(1)}, s32[3,2048]{1,0:T(4,128)}, u32[]{:S(2)}) copy-start(s32[3,2048]{1,0:T(4,128)} %param.9) | copy-start | bytes 73732
  224.6 22.9 %copy-start.2 = (s32[128]{0:T(128)S(1)}, s32[128]{0:T(128)}, u32[]{:S(2)}) copy-start(s32[128]{0:T(128)} %param.10) | copy-start | bytes 1540
  240.1 37.7 %all-to-all-start.4 = ((f32[384,3,384]{2,1,0:T(4,128)}), f32[384,3,384]{2,1,0:T(4,128)}, u32[]{:S(2)}, u32[]{:S(2)}) async-start(f32[384,3,384]{2,1,0:T(4,128)} %copy.110), calls=%async_computation.4 | async-start | bytes 4718592 | tf_op jit(solution)/shard_map/all_to_all | solution.py:238
  297.9 36.0 %all-to-all-start.7 = ((f32[3,384,384]{2,0,1:T(4,128)}), f32[3,384,384]{2,0,1:T(4,128)}, u32[]{:S(2)}, u32[]{:S(2)}) async-start(f32[3,384,384]{2,0,1:T(4,128)} %copy.124), calls=%async_computation.7 | async-start | bytes 4718592 | tf_op jit(solution)/shard_map/all_to_all | solution.py:244
  306.4 34.4 %copy-start.11 = (f32[34,10]{0,1:T(8,128)}, f32[34,10]{0,1:T(8,128)S(1)}, u32[]{:S(2)}) copy-start(f32[34,10]{0,1:T(8,128)S(1)} %select_add_fusion) | copy-start | bytes 4084
  322.5 18.4 %copy-start.26 = (s32[2,16]{1,0:T(2,128)S(1)}, s32[2,16]{1,0:T(2,128)}, u32[]{:S(2)}) copy-start(s32[2,16]{1,0:T(2,128)} %constant_dynamic-slice_fusion) | copy-start | bytes 388
  322.5 19.0 %copy-start.29 = (s32[16]{0:T(128)S(1)}, s32[16]{0:T(128)}, u32[]{:S(2)}) copy-start(s32[16]{0:T(128)} %get-tuple-element.5) | copy-start | bytes 196
  322.5 19.0 %copy-start.28 = (s32[16]{0:T(128)S(1)}, s32[16]{0:T(128)}, u32[]{:S(2)}) copy-start(s32[16]{0:T(128)} %get-tuple-element.6) | copy-start | bytes 196
  322.5 19.1 %copy-start.27 = (s32[16]{0:T(128)S(1)}, s32[16]{0:T(128)}, u32[]{:S(2)}) copy-start(s32[16]{0:T(128)} %get-tuple-element.7) | copy-start | bytes 196
  322.5 19.2 %copy-start.22 = (f32[10]{0:T(128)S(1)}, f32[10]{0:T(128)}, u32[]{:S(2)}) copy-start(f32[10]{0:T(128)} %get-tuple-element.4) | copy-start | bytes 124
  322.5 19.2 %copy-start.24 = (f32[10]{0:T(128)S(1)}, f32[10]{0:T(128)}, u32[]{:S(2)}) copy-start(f32[10]{0:T(128)} %get-tuple-element.3) | copy-start | bytes 124
  333.9 35.2 %all-to-all-start.6 = ((f32[3,384,384]{2,0,1:T(4,128)}), f32[3,384,384]{2,0,1:T(4,128)S(1)}, u32[]{:S(2)}, u32[]{:S(2)}) async-start(f32[3,384,384]{2,0,1:T(4,128)} %copy.120), calls=%async_computation.6 | async-start | bytes 4718592 | tf_op jit(solution)/shard_map/all_to_all | solution.py:243
  369.1 5.8 copy-start.10
  380.9 10.1 %copy-start.5 = (f32[48,24,384]{2,1,0:T(8,128)}, f32[48,24,384]{2,1,0:T(8,128)S(1)}, u32[]{:S(2)}) copy-start(f32[48,24,384]{2,1,0:T(8,128)S(1)} %subtract_multiply_fusion) | copy-start | bytes 5308420
  380.9 5.4 collective-permute-start
  381.0 5.4 collective-permute-start.1
  386.5 4.5 collective-permute-start.2
  387.5 6.5 collective-permute-start.3
  395.8 151.7 %copy-start.30 = (pred[16]{0:T(512)(128)(4,1)S(1)}, pred[16]{0:T(512)(128)(4,1)}, u32[]{:S(2)}) copy-start(pred[16]{0:T(512)(128)(4,1)} %fusion.227) | copy-start | bytes 52
  395.8 175.8 %copy-start.3 = (s32[128]{0:T(128)S(1)}, s32[128]{0:T(128)}, u32[]{:S(2)}) copy-start(s32[128]{0:T(128)} %param.10) | copy-start | bytes 1540
  395.8 184.5 %copy-start.16 = (f32[32,10,10]{0,1,2:T(8,128)S(1)}, f32[32,10,10]{0,1,2:T(8,128)}, u32[]{:S(2)}) copy-start(f32[32,10,10]{0,1,2:T(8,128)} %get-tuple-element.78) | copy-start | bytes 38404
  395.8 184.5 %copy-start.15 = (f32[32,10,10]{0,2,1:T(8,128)S(1)}, f32[32,10,10]{0,2,1:T(8,128)}, u32[]{:S(2)}) copy-start(f32[32,10,10]{0,2,1:T(8,128)} %get-tuple-element.79) | copy-start | bytes 38404
  395.8 184.5 %copy-start.14 = (f32[32,10,10]{0,2,1:T(8,128)S(1)}, f32[32,10,10]{0,2,1:T(8,128)}, u32[]{:S(2)}) copy-start(f32[32,10,10]{0,2,1:T(8,128)} %get-tuple-element.82) | copy-start | bytes 38404
  395.9 184.5 %copy-start.13 = (f32[32,10,10]{0,1,2:T(8,128)S(1)}, f32[32,10,10]{0,1,2:T(8,128)}, u32[]{:S(2)}) copy-start(f32[32,10,10]{0,1,2:T(8,128)} %get-tuple-element.83) | copy-start | bytes 38404
  547.6 11.0 %collective-permute-start.18 = (f32[1,1000]{1,0:T(1,128)S(1)}, f32[1,1000]{1,0:T(1,128)S(1)}, u32[]{:S(2)}, u32[]{:S(2)}) collective-permute-start(f32[1,1000]{1,0:T(1,128)S(1)} %get-tuple-element.62), channel_id=1, source_target_pairs={{0,15},{1,14},{2,13},{3,12},{4,11},{5,10},{6,9},{7,8},{8,7},{9,6},... | collective-permute-start | bytes 12008 | tf_op jit(solution)/shard_map/ppermute | solution.py:267
  549.1 14.6 %collective-permute-start.17 = (f32[1,1000]{1,0:T(1,128)S(1)}, f32[1,1000]{1,0:T(1,128)S(1)}, u32[]{:S(2)}, u32[]{:S(2)}) collective-permute-start(f32[1,1000]{1,0:T(1,128)S(1)} %get-tuple-element.63), channel_id=1, source_target_pairs={{0,14},{1,15},{2,12},{3,13},{4,10},{5,11},{6,8},{7,9},{8,6},{9,7},... | collective-permute-start | bytes 12008 | tf_op jit(solution)/shard_map/ppermute | solution.py:267
  550.9 12.8 %collective-permute-start.16 = (f32[1,1000]{1,0:T(1,128)S(1)}, f32[1,1000]{1,0:T(1,128)S(1)}, u32[]{:S(2)}, u32[]{:S(2)}) collective-permute-start(f32[1,1000]{1,0:T(1,128)S(1)} %get-tuple-element.64), channel_id=1, source_target_pairs={{0,13},{1,12},{2,15},{3,14},{4,9},{5,8},{6,11},{7,10},{8,5},{9,4},... | collective-permute-start | bytes 12008 | tf_op jit(solution)/shard_map/ppermute | solution.py:267
  558.6 9.5 %collective-permute-start.15 = (f32[1,1000]{1,0:T(1,128)S(1)}, f32[1,1000]{1,0:T(1,128)S(1)}, u32[]{:S(2)}, u32[]{:S(2)}) collective-permute-start(f32[1,1000]{1,0:T(1,128)S(1)} %get-tuple-element.65), channel_id=1, source_target_pairs={{0,12},{1,13},{2,14},{3,15},{4,8},{5,9},{6,10},{7,11},{8,4},{9,5},... | collective-permute-start | bytes 12008 | tf_op jit(solution)/shard_map/ppermute | solution.py:267
  558.6 10.1 %collective-permute-start.14 = (f32[1,1000]{1,0:T(1,128)S(1)}, f32[1,1000]{1,0:T(1,128)S(1)}, u32[]{:S(2)}, u32[]{:S(2)}) collective-permute-start(f32[1,1000]{1,0:T(1,128)S(1)} %get-tuple-element.66), channel_id=1, source_target_pairs={{0,11},{1,10},{2,9},{3,8},{4,15},{5,14},{6,13},{7,12},{8,3},{9,2},... | collective-permute-start | bytes 12008 | tf_op jit(solution)/shard_map/ppermute | solution.py:267
  558.7 13.6 %collective-permute-start.13 = (f32[1,1000]{1,0:T(1,128)S(1)}, f32[1,1000]{1,0:T(1,128)S(1)}, u32[]{:S(2)}, u32[]{:S(2)}) collective-permute-start(f32[1,1000]{1,0:T(1,128)S(1)} %get-tuple-element.67), channel_id=1, source_target_pairs={{0,10},{1,11},{2,8},{3,9},{4,14},{5,15},{6,12},{7,13},{8,2},{9,3},... | collective-permute-start | bytes 12008 | tf_op jit(solution)/shard_map/ppermute | solution.py:267
  563.7 10.1 %collective-permute-start.12 = (f32[1,1000]{1,0:T(1,128)S(1)}, f32[1,1000]{1,0:T(1,128)S(1)}, u32[]{:S(2)}, u32[]{:S(2)}) collective-permute-start(f32[1,1000]{1,0:T(1,128)S(1)} %get-tuple-element.68), channel_id=1, source_target_pairs={{0,9},{1,8},{2,11},{3,10},{4,13},{5,12},{6,15},{7,14},{8,1},{9,0},... | collective-permute-start | bytes 12008 | tf_op jit(solution)/shard_map/ppermute | solution.py:267
  563.7 11.5 %collective-permute-start.11 = (f32[1,1000]{1,0:T(1,128)S(1)}, f32[1,1000]{1,0:T(1,128)S(1)}, u32[]{:S(2)}, u32[]{:S(2)}) collective-permute-start(f32[1,1000]{1,0:T(1,128)S(1)} %get-tuple-element.69), channel_id=1, source_target_pairs={{0,8},{1,9},{2,10},{3,11},{4,12},{5,13},{6,14},{7,15},{8,0},{9,1},... | collective-permute-start | bytes 12008 | tf_op jit(solution)/shard_map/ppermute | solution.py:267
  568.1 7.7 %collective-permute-start.10 = (f32[1,1000]{1,0:T(1,128)S(1)}, f32[1,1000]{1,0:T(1,128)S(1)}, u32[]{:S(2)}, u32[]{:S(2)}) collective-permute-start(f32[1,1000]{1,0:T(1,128)S(1)} %get-tuple-element.70), channel_id=1, source_target_pairs={{0,7},{1,6},{2,5},{3,4},{4,3},{5,2},{6,1},{7,0},{8,15},{9,14},{10,... | collective-permute-start | bytes 12008 | tf_op jit(solution)/shard_map/ppermute | solution.py:267
  568.8 9.1 %collective-permute-start.9 = (f32[1,1000]{1,0:T(1,128)S(1)}, f32[1,1000]{1,0:T(1,128)S(1)}, u32[]{:S(2)}, u32[]{:S(2)}) collective-permute-start(f32[1,1000]{1,0:T(1,128)S(1)} %get-tuple-element.71), channel_id=1, source_target_pairs={{0,6},{1,7},{2,4},{3,5},{4,2},{5,3},{6,0},{7,1},{8,14},{9,15},{10,... | collective-permute-start | bytes 12008 | tf_op jit(solution)/shard_map/ppermute | solution.py:267
  572.3 10.4 %collective-permute-start.8 = (f32[1,1000]{1,0:T(1,128)S(1)}, f32[1,1000]{1,0:T(1,128)S(1)}, u32[]{:S(2)}, u32[]{:S(2)}) collective-permute-start(f32[1,1000]{1,0:T(1,128)S(1)} %get-tuple-element.72), channel_id=1, source_target_pairs={{0,5},{1,4},{2,7},{3,6},{4,1},{5,0},{6,3},{7,2},{8,13},{9,12},{10,... | collective-permute-start | bytes 12008 | tf_op jit(solution)/shard_map/ppermute | solution.py:267
  573.8 8.9 %collective-permute-start.7 = (f32[1,1000]{1,0:T(1,128)S(1)}, f32[1,1000]{1,0:T(1,128)S(1)}, u32[]{:S(2)}, u32[]{:S(2)}) collective-permute-start(f32[1,1000]{1,0:T(1,128)S(1)} %get-tuple-element.73), channel_id=1, source_target_pairs={{0,4},{1,5},{2,6},{3,7},{4,0},{5,1},{6,2},{7,3},{8,12},{9,13},{10,... | collective-permute-start | bytes 12008 | tf_op jit(solution)/shard_map/ppermute | solution.py:267
  575.2 7.5 %collective-permute-start.6 = (f32[1,1000]{1,0:T(1,128)S(1)}, f32[1,1000]{1,0:T(1,128)S(1)}, u32[]{:S(2)}, u32[]{:S(2)}) collective-permute-start(f32[1,1000]{1,0:T(1,128)S(1)} %get-tuple-element.74), channel_id=1, source_target_pairs={{0,3},{1,2},{2,1},{3,0},{4,7},{5,6},{6,5},{7,4},{8,11},{9,10},{10,... | collective-permute-start | bytes 12008 | tf_op jit(solution)/shard_map/ppermute | solution.py:267
  575.8 6.9 collective-permute-start.5
  577.8 4.9 collective-permute-start.4
  593.2 11.6 %copy-start.20 = (pred[16]{0:T(512)(128)(4,1)S(1)}, pred[16]{0:T(512)(128)(4,1)}, u32[]{:S(2)}) copy-start(pred[16]{0:T(512)(128)(4,1)} %get-tuple-element.84) | copy-start | bytes 52
  594.2 13.6 %copy-start.21 = (pred[16]{0:T(512)(128)(4,1)S(1)}, pred[16]{0:T(512)(128)(4,1)}, u32[]{:S(2)}) copy-start(pred[16]{0:T(512)(128)(4,1)} %get-tuple-element.85) | copy-start | bytes 52
  594.2 14.1 %copy-start.4 = (f32[16,32,1024]{2,1,0:T(8,128)S(1)}, f32[16,32,1024]{2,1,0:T(8,128)}, u32[]{:S(2)}) copy-start(f32[16,32,1024]{2,1,0:T(8,128)} %param.7) | copy-start | bytes 6291460
  594.2 14.1 %copy-start.17 = (pred[1024]{0:T(1024)(128)(4,1)S(1)}, pred[1024]{0:T(1024)(128)(4,1)}, u32[]{:S(2)}) copy-start(pred[1024]{0:T(1024)(128)(4,1)} %get-tuple-element.93) | copy-start | bytes 3076
  594.2 14.1 %copy-start.18 = (pred[1024]{0:T(1024)(128)(4,1)S(1)}, pred[1024]{0:T(1024)(128)(4,1)}, u32[]{:S(2)}) copy-start(pred[1024]{0:T(1024)(128)(4,1)} %get-tuple-element.94) | copy-start | bytes 3076
  594.2 10.5 %collective-permute-start.19 = (f32[16,32,32]{2,1,0:T(8,128)S(1)}, f32[16,32,32]{2,1,0:T(8,128)S(1)}, u32[]{:S(2)}, u32[]{:S(2)}) collective-permute-start(f32[16,32,32]{2,1,0:T(8,128)S(1)} %get-tuple-element.50), channel_id=1, source_target_pairs={{1,0},{2,1},{3,2},{4,3},{5,4},{6,5},{7,6},{8,7},{9,8},{10,9},{11,1... | collective-permute-start | bytes 196616 | tf_op jit(solution)/shard_map/ppermute | solution.py:29
  598.4 9.4 %collective-permute-start.20 = (f32[16,32,32]{2,1,0:T(8,128)S(1)}, f32[16,32,32]{2,1,0:T(8,128)S(1)}, u32[]{:S(2)}, u32[]{:S(2)}) collective-permute-start(f32[16,32,32]{2,1,0:T(8,128)S(1)} %get-tuple-element.51), channel_id=1, source_target_pairs={{0,1},{1,2},{2,3},{3,4},{4,5},{5,6},{6,7},{7,8},{8,9},{9,10},{10,1... | collective-permute-start | bytes 196616 | tf_op jit(solution)/shard_map/ppermute | solution.py:29
  612.6 10.4 %collective-permute-start.22 = (f32[16,32,32]{2,1,0:T(8,128)S(1)}, f32[16,32,32]{2,1,0:T(8,128)S(1)}, u32[]{:S(2)}, u32[]{:S(2)}) collective-permute-start(f32[16,32,32]{2,1,0:T(8,128)S(1)} %get-tuple-element.40), channel_id=1, source_target_pairs={{0,1},{1,2},{2,3},{3,4},{4,5},{5,6},{6,7},{7,8},{8,9},{9,10},{10,1... | collective-permute-start | bytes 196616 | tf_op jit(solution)/shard_map/ppermute | solution.py:29
  619.9 10.4 %collective-permute-start.21 = (f32[16,32,32]{2,1,0:T(8,128)S(1)}, f32[16,32,32]{2,1,0:T(8,128)S(1)}, u32[]{:S(2)}, u32[]{:S(2)}) collective-permute-start(f32[16,32,32]{2,1,0:T(8,128)S(1)} %get-tuple-element.41), channel_id=1, source_target_pairs={{1,0},{2,1},{3,2},{4,3},{5,4},{6,5},{7,6},{8,7},{9,8},{10,9},{11,1... | collective-permute-start | bytes 196616 | tf_op jit(solution)/shard_map/ppermute | solution.py:29
  635.1 10.4 %collective-permute-start.23 = (f32[16,32,32]{2,1,0:T(8,128)S(1)}, f32[16,32,32]{2,1,0:T(8,128)S(1)}, u32[]{:S(2)}, u32[]{:S(2)}) collective-permute-start(f32[16,32,32]{2,1,0:T(8,128)S(1)} %get-tuple-element.34), channel_id=1, source_target_pairs={{1,0},{2,1},{3,2},{4,3},{5,4},{6,5},{7,6},{8,7},{9,8},{10,9},{11,1... | collective-permute-start | bytes 196616 | tf_op jit(solution)/shard_map/ppermute | solution.py:29
  637.5 9.9 %collective-permute-start.24 = (f32[16,32,32]{2,1,0:T(8,128)S(1)}, f32[16,32,32]{2,1,0:T(8,128)S(1)}, u32[]{:S(2)}, u32[]{:S(2)}) collective-permute-start(f32[16,32,32]{2,1,0:T(8,128)S(1)} %get-tuple-element.35), channel_id=1, source_target_pairs={{0,1},{1,2},{2,3},{3,4},{4,5},{5,6},{6,7},{7,8},{8,9},{9,10},{10,1... | collective-permute-start | bytes 196616 | tf_op jit(solution)/shard_map/ppermute | solution.py:29
  651.9 10.8 %collective-permute-start.25 = (f32[16,32,32]{2,1,0:T(8,128)S(1)}, f32[16,32,32]{2,1,0:T(8,128)S(1)}, u32[]{:S(2)}, u32[]{:S(2)}) collective-permute-start(f32[16,32,32]{2,1,0:T(8,128)S(1)} %get-tuple-element.26), channel_id=1, source_target_pairs={{1,0},{2,1},{3,2},{4,3},{5,4},{6,5},{7,6},{8,7},{9,8},{10,9},{11,1... | collective-permute-start | bytes 196616 | tf_op jit(solution)/shard_map/ppermute | solution.py:29
  654.6 10.4 %collective-permute-start.26 = (f32[16,32,32]{2,1,0:T(8,128)S(1)}, f32[16,32,32]{2,1,0:T(8,128)S(1)}, u32[]{:S(2)}, u32[]{:S(2)}) collective-permute-start(f32[16,32,32]{2,1,0:T(8,128)S(1)} %get-tuple-element.27), channel_id=1, source_target_pairs={{0,1},{1,2},{2,3},{3,4},{4,5},{5,6},{6,7},{7,8},{8,9},{9,10},{10,1... | collective-permute-start | bytes 196616 | tf_op jit(solution)/shard_map/ppermute | solution.py:29
  671.3 10.4 %collective-permute-start.28 = (f32[16,32,32]{2,1,0:T(8,128)S(1)}, f32[16,32,32]{2,1,0:T(8,128)S(1)}, u32[]{:S(2)}, u32[]{:S(2)}) collective-permute-start(f32[16,32,32]{2,1,0:T(8,128)S(1)} %get-tuple-element.16), channel_id=1, source_target_pairs={{0,1},{1,2},{2,3},{3,4},{4,5},{5,6},{6,7},{7,8},{8,9},{9,10},{10,1... | collective-permute-start | bytes 196616 | tf_op jit(solution)/shard_map/ppermute | solution.py:29
  677.9 10.4 %collective-permute-start.27 = (f32[16,32,32]{2,1,0:T(8,128)S(1)}, f32[16,32,32]{2,1,0:T(8,128)S(1)}, u32[]{:S(2)}, u32[]{:S(2)}) collective-permute-start(f32[16,32,32]{2,1,0:T(8,128)S(1)} %get-tuple-element.17), channel_id=1, source_target_pairs={{1,0},{2,1},{3,2},{4,3},{5,4},{6,5},{7,6},{8,7},{9,8},{10,9},{11,1... | collective-permute-start | bytes 196616 | tf_op jit(solution)/shard_map/ppermute | solution.py:29
  680.8 8.2 %slice-start = ((s8[6291456]{0:T(1024)(128)(4,1)}), s8[4194304]{0:T(1024)(128)(4,1)S(1)}, s32[]{:S(2)}) async-start(s8[6291456]{0:T(1024)(128)(4,1)} %bitcast.272), calls=%async_computation.8 | async-start | bytes 8388608
  681.8 7.2 %slice-start.1 = ((s8[6291456]{0:T(1024)(128)(4,1)}), s8[2097152]{0:T(1024)(128)(4,1)S(1)}, s32[]{:S(2)}) async-start(s8[6291456]{0:T(1024)(128)(4,1)} %bitcast.272), calls=%async_computation.9 | async-start | bytes 4194304
  (6 other events, 23.2 us)
